TPU v7x, 256 devices: a whole 4x4x8 slice. The times are simulated.
256 devices in a mesh: seg: 16 (over z, core), head: 16 (over x, y).
Axes of the slice: x: 4, y: 4, z: 8, core: 2. Of those that a mesh axis runs over, the one named last changes fastest.
Arguments:
- inputs: bfloat16 [16, 256, 16384], P('seg', None, 'head'), may hold values from -6 to 6
- deltas: float32 [16, 256, 256], P('seg', 'head'), may hold values from 0.01 to 0.1
- rates: float32 [256], P('head'), may hold values from 0.001 to 2
- skips: float32 [256], P('head'), may hold values from 0.5 to 1.5
- writer: bfloat16 [16, 256, 1024], P('seg'), may hold values from -1.796875 to 1.796875
- reader: bfloat16 [16, 256, 1024], P('seg'), may hold values from -1.796875 to 1.796875
- grad_out: bfloat16 [16, 256, 16384], P('seg', None, 'head'), may hold values from -6 to 6
- parents: int32 [16], replicated, may hold values from -1 to 15, as said below
- levels: int32 [16], replicated, may hold values from 0 to 2, as said below
Outputs:
- outputs: bfloat16 [16, 256, 16384], P('seg', None, 'head')
- grad_inputs: bfloat16 [16, 256, 16384], P('seg', None, 'head')
- grad_deltas: float32 [16, 256, 256], P('seg', 'head')
- grad_writer: bfloat16 [16, 256, 1024], P('seg', 'head')
- grad_reader: bfloat16 [16, 256, 1024], P('seg', 'head')
Inputs may be any that keep to these rules, and one draw needn't show every extreme that they name: `parents`: roots have parent -1 and level 0; every other segment's parent has a level one less than its own. A segment has at most four children, and some segment has level 2. levels[s] is the number of ancestors of segment s.
All inputs are finite; a program needn't handle non-finite values.
Results may differ from a plain program's by a relative error of at most 0.0046.
Values may be sent and summed in bfloat16 or wider, within the bound.
A program may use at most 128 MiB of HBM per device.

v0:
```python
import jax
import jax.numpy as jnp
from jax import lax
from jax.sharding import PartitionSpec as P

H = 256
P_SIZE = 64
N = 128
G = 8
BLOCK = 256
DEPTH = 3


exact_mode = lax.Precision.HIGHEST


def sent_together(arrays, axis, dim, along):
    columns = [a.reshape(*a.shape[:along], -1) for a in arrays]
    both = jnp.concatenate(columns, axis=along)
    result, at, done = (lax.all_gather(both, axis, axis=dim, tiled=True), 0, [])
    for a, column in zip(arrays, columns):
        piece = result[..., at : at + column.shape[along]]
        done.append(piece.reshape(*piece.shape[:along], *a.shape[along:]))
        at += column.shape[along]
    return tuple(done)


def sent_together_2(arrays, axis, split_dim, concat_dim, along):
    ends, at = ([], 0)
    for a in arrays[:-1]:
        at += a.shape[along]
        ends.append(at)
    both = jnp.concatenate(arrays, axis=along)
    return tuple(
        jnp.split(
            lax.all_to_all(both, axis, split_axis=split_dim, concat_axis=concat_dim, tiled=True),
            ends,
            axis=along,
        )
    )


def round_half(values):
    return lax.optimization_barrier(values.astype(jnp.bfloat16)).astype(jnp.float32)


def ssd_forward(values, deltas, rates, writer, reader, start, block):
    length, groups, per_group, width = values.shape
    state_size = writer.shape[-1]
    blocks = length // block
    log_decay = (-rates[:, :, None] * deltas).reshape(groups, per_group, blocks, block)
    within = jnp.cumsum(log_decay, axis=-1)
    value_blk = values.reshape(blocks, block, groups, per_group, width)
    write_blk = writer.reshape(blocks, block, groups, state_size)
    read_blk = reader.reshape(blocks, block, groups, state_size)
    delta_blk = deltas.reshape(groups, per_group, blocks, block)
    scores = jnp.einsum("cign,cjgn->gcij", read_blk, write_blk, precision=exact_mode)
    positions = jnp.arange(block)
    causal = positions[:, None] >= positions[None, :]
    log_gap = within[..., :, None] - within[..., None, :]
    decays = jnp.exp(jnp.where(causal, log_gap, -jnp.inf))
    weights = scores[:, None] * decays * delta_blk[..., None, :]
    within_out = jnp.einsum("ghcij,cjghp->cighp", weights, value_blk, precision=exact_mode)
    tail_decay = jnp.exp(within[..., -1:] - within) * delta_blk
    local_state = jnp.einsum(
        "ghcj,cjghp,cjgn->cghpn", tail_decay, value_blk, write_blk, precision=exact_mode
    )
    totals = jnp.exp(within[..., -1])
    current = start
    read_out = jnp.einsum("ign,ghpn->ighp", read_blk[0], current, precision=exact_mode)
    scale_in = jnp.transpose(jnp.exp(within[:, :, 0, :]), (2, 0, 1))
    outer_terms = [read_out * scale_in[..., None]]
    current = totals[:, :, 0, None, None] * current + local_state[0]
    output = within_out + jnp.stack(outer_terms)
    return (output.reshape(length, groups, per_group, width), current)


def segment_end(values, deltas, rates, writer):
    running = jnp.cumsum(-rates[:, :, None] * deltas, axis=-1)
    total = running[..., -1]
    tail_decay = jnp.exp(total[..., None] - running) * deltas
    local_state = jnp.einsum("ghj,jghp,jgn->ghpn", tail_decay, values, writer, precision=exact_mode)
    return (local_state, jnp.exp(total))


def start_grad(grads, deltas, rates, reader):
    running = jnp.cumsum(-rates[:, :, None] * deltas, axis=-1)
    return jnp.einsum("ghi,ighp,ign->ghpn", jnp.exp(running), grads, reader, precision=exact_mode)


def shards(inputs, deltas, rates, skips, writer, reader, grad_out, parents, levels):
    length = inputs.shape[1]
    heads = deltas.shape[1]
    per_group_all = H // G
    local_groups = max(1, heads // per_group_all)
    per_group = heads // local_groups
    first_group = lax.axis_index("head") * heads // per_group_all
    own_slot = lax.axis_index("seg")
    rate_grid = rates.reshape(local_groups, per_group)
    skip_grid = skips.reshape(local_groups, per_group)
    values = inputs[0].astype(jnp.float32).reshape(length, local_groups, per_group, P_SIZE)
    delta_one = deltas[0].reshape(local_groups, per_group, length)
    write_one = lax.dynamic_slice_in_dim(
        writer[0].reshape(length, G, N), first_group, local_groups, 1
    ).astype(jnp.float32)
    read_one = lax.dynamic_slice_in_dim(
        reader[0].reshape(length, G, N), first_group, local_groups, 1
    ).astype(jnp.float32)
    grads = grad_out[0].astype(jnp.float32).reshape(length, local_groups, per_group, P_SIZE)
    local_state, decay_all = segment_end(values, delta_one, rate_grid, write_one)
    start_part = start_grad(grads, delta_one, rate_grid, read_one)
    safe_parent = jnp.maximum(parents, 0)
    own_level = levels[own_slot]
    starts = jnp.zeros_like(local_state)
    gathered, gathered_decay = sent_together((local_state[None], decay_all[None]), "seg", 0, 3)
    for distance in range(DEPTH - 1, 0, -1):
        ancestor = own_slot
        for repeat in range(distance):
            ancestor = safe_parent[ancestor]
        end_state = round_half(
            gathered_decay[ancestor][..., None, None] * starts + gathered[ancestor]
        )
        starts = jnp.where(distance <= own_level, end_state, starts)
    gathered_part, gathered_decay = (
        lax.all_gather(start_part[None], "seg", axis=0, tiled=True),
        lax.all_gather(decay_all[None], "seg", axis=0, tiled=True),
    )
    upward = parents
    carried = jnp.ones_like(gathered_decay)
    factors = jnp.zeros_like(gathered_decay)
    for repeat in range(DEPTH - 1):
        factors = factors + jnp.where((upward == own_slot)[:, None, None], carried, 0.0)
        lifted = jnp.maximum(upward, 0)
        carried = carried * gathered_decay[lifted]
        upward = jnp.where(upward < 0, -1, parents[lifted])
    grad_end = jnp.einsum("dgh,dghpn->ghpn", factors, gathered_part, precision=exact_mode)

    def core_map(values, delta_one, write_one, read_one):
        return ssd_forward(values, delta_one, rate_grid, write_one, read_one, starts, BLOCK)

    (core_out, end_state), pullback = jax.vjp(core_map, values, delta_one, write_one, read_one)
    grad_values, grad_delta, grad_write, grad_read = pullback((grads, grad_end))
    result = core_out + skip_grid[None, :, :, None] * values
    grad_values = grad_values + skip_grid[None, :, :, None] * grads
    owners = lax.axis_size("head")
    rows_each = length // owners
    write_parts = grad_write.reshape(owners, rows_each, local_groups * N)
    read_parts = grad_read.reshape(owners, rows_each, local_groups * N)
    came_write, came_read = sent_together_2((write_parts, read_parts), "head", 0, 0, 1)
    source = jnp.arange(owners, dtype=jnp.int32)[:, None, None]
    offset = jnp.arange(local_groups, dtype=jnp.int32)[None, :, None]
    column = jnp.arange(G, dtype=jnp.int32)[None, None, :]
    placing = (source * heads // per_group_all + offset == column).astype(jnp.float32)
    summed_write = jnp.einsum(
        "dbkn,dkg->bgn",
        came_write.reshape(owners, rows_each, local_groups, N),
        placing,
        precision=exact_mode,
    ).reshape(rows_each, G * N)
    summed_read = jnp.einsum(
        "dbkn,dkg->bgn",
        came_read.reshape(owners, rows_each, local_groups, N),
        placing,
        precision=exact_mode,
    ).reshape(rows_each, G * N)
    return (
        result.reshape(1, length, heads * P_SIZE).astype(jnp.bfloat16),
        grad_values.reshape(1, length, heads * P_SIZE).astype(jnp.bfloat16),
        grad_delta,
        summed_write.astype(jnp.bfloat16)[None],
        summed_read.astype(jnp.bfloat16)[None],
    )


def solution(mesh):
    placed = (
        P("seg", None, "head"),
        P("seg", "head", None),
        P("head"),
        P("head"),
        P("seg", None, None),
        P("seg", None, None),
        P("seg", None, "head"),
        P(),
        P(),
    )
    return jax.shard_map(
        shards,
        mesh=mesh,
        in_specs=placed,
        out_specs=(
            P("seg", None, "head"),
            P("seg", None, "head"),
            P("seg", "head", None),
            P("seg", "head", None),
            P("seg", "head", None),
        ),
        check_vma=False,
    )
```

profile of v0, /device:TPU:1, one launch (start us, length us, event | category | flops | bytes accessed | tf_op | source)
XLA Modules:
  0.0 191.8 jit_solution(3838290157942920395)
XLA Ops:
  7.3 0.7 neg.14
  8.0 0.8 copy.208
  8.9 0.6 reduce-window.24
  9.5 0.2 slice_reduce_fusion.1
  9.8 1.2 copy.224
  11.1 1.1 copy.258
  12.2 0.1 constant_dynamic-slice_fusion.1
  12.6 1.4 fusion.43
  14.1 0.3 slice_reduce_fusion.3
  14.5 0.6 copy.276
  15.1 0.2 copy.212
  15.4 0.1 constant_dynamic-slice_fusion
  15.6 1.4 fusion.37
  17.1 0.9 pad_maximum_fusion
  18.0 0.6 dynamic_slice.31
  20.5 0.6 dynamic_slice.33
  22.5 0.6 reduce-window.20
  23.1 0.6 copy.210
  23.8 1.2 dynamic_slice.30
  26.3 0.7 gather_fusion
  27.2 0.2 slice_reduce_fusion.2
  27.3 21.2 %all-gather = f32[16,16,1]{1,2,0:T(1,128)S(1)} all-gather(f32[1,16,1]{1,2,0:T(1,128)S(1)} %copy.222), channel_id=2, replica_groups=mesh['seg'=16,'head'=16] {'seg'}, dimensions={0}, use_global_device_ids=true | all-gather | bytes 1088 | tf_op jit(solution)/shard_map/all_gather | solution.py:126
  48.5 0.6 gather_fusion.1
  49.3 0.8 copy.219
  50.2 0.7 copy.252
  51.5 0.6 and_select_fusion
  52.1 0.7 iota_compare_fusion
  52.8 0.9 fusion.78
  53.7 20.7 %all-gather.7.cloned.1.call-done = f32[256,64,128]{2,1,0:T(8,128)} async-done(((f32[16,64,128]{2,1,0:T(8,128)}), f32[256,64,128]{2,1,0:T(8,128)}) %all-gather.7.cloned.1.call-update) | async-done | bytes 8388624 | tf_op jit(solution)/shard_map/all_gather | solution.py:125
  74.4 12.5 %fusion = f32[16,1,64,128]{3,1,2,0:T(1,128)S(1)} fusion(f32[16,16,1,1]{0,2,3,1:T(1,128)S(1)} %copy.243, f32[16,16,64,128]{3,2,1,0:T(8,128)} %bitcast.277), kind=kOutput, calls=%fused_computation.2 | convolution fusion | flops 25165824 | bytes 8913920 | tf_op jit(solution)/shard_map/dgh,dghpn->ghpn/dot_general | solution.py:136
  86.8 1.6 fusion.38
  88.6 42.7 %all-gather.5.cloned.1.call-done = f32[16,1,16,8193]{3,2,1,0:T(8,128)} async-done(((f32[1,1,16,8193]{3,2,1,0:T(8,128)}), f32[16,1,16,8193]{3,2,1,0:T(8,128)}) %all-gather.5.cloned.1.call-update) | async-done | bytes 8389648 | tf_op jit(solution)/shard_map/all_gather | solution.py:20
  131.3 3.4 %slice-done = f32[16,1,16,8192]{3,2,1,0:T(8,128)S(1)} async-done(((f32[16,1,16,8193]{3,2,1,0:T(8,128)}), f32[16,1,16,8192]{3,2,1,0:T(8,128)S(1)}, s32[]{:S(2)}) %slice-start) | async-done | bytes 8388632 | tf_op jit(solution)/shard_map/slice | solution.py:22
  134.7 1.6 copy.261
  136.4 0.1 dynamic-slice_reduce_fusion
  136.6 0.1 fusion.47
  136.7 0.2 multiply_reduce_fusion.3
  137.1 1.1 convolution_bitcast_fusion.4
  138.2 3.6 %fusion.9 = (f32[16,256]{1,0:T(8,128)}, f32[16,256]{1,0:T(8,128)}, f32[16,256]{1,0:T(8,128)}, f32[256,256]{1,0:T(8,128)S(1)}) fusion(f32[16,256]{1,0:T(8,128)S(1)} %bitcast.297, f32[16,256]{1,0:T(8,128)S(1)} %get-tuple-element.51, f32[256,256]{1,0:T(8,128)S(1)} %copy-done.8, pred[256,256]{1,0:T(8,128)(4,1)S(1)} %copy-done.17, ...), kind=kOutput, calls=%fused_computation.13 | convolution fusion | flops 147771392 | bytes 1720320 | tf_op jit(solution)/shard_map/transpose(jvp(ghcij,cjghp->cighp))/dot_general | solution.py:63
  141.8 0.9 fusion.34
  142.7 1.7 copy.237
  144.3 1.5 copy.231
  145.8 1.5 copy.232
  147.3 1.2 fusion.95
  148.5 1.6 multiply_reduce_fusion.2
  150.1 0.8 copy.229
  150.8 1.8 fusion.66
  152.6 1.0 copy.233
  153.6 2.7 %reduce-window.26 = f32[1,16,1,2,128]{4,1,2,3,0:T(8,128)S(1)} reduce-window(f32[1,16,1,2,128]{4,1,2,3,0:T(8,128)S(1)} %copy.233, f32[]{:T(128)} %constant.63.clone.1), window={size=1x1x1x1x128 pad=0_0x0_0x0_0x0_0x0_127}, to_apply=%region_10.11 | reduce-window | flops 520192 | bytes 32772 | tf_op jit(solution)/shard_map/reduce-window.4
  156.4 1.8 convolution_bitcast_fusion.3
  158.2 0.3 convolution_add_fusion
  158.5 5.8 %fusion.31 = f32[1,256,1,16,64]{1,4,3,2,0:T(8,128)} fusion(bf16[256,16,64]{0,2,1:T(8,128)(2,1)S(1)} %bitcast.274, f32[16,256]{1,0:T(8,128)} %bitcast.296, f32[16,256]{1,0:T(8,128)} %copy-done.20, f32[256,256]{1,0:T(8,128)} %fusion.78, pred[256,256]{1,0:T(8,128)(4,1)} %iota_compare_fusion, f32[256,1,16,64]{0,3,2,1:T(8,128)} %get-tuple-element.61, ...), kind=kOutput, calls=%fused_computation.34 | convolution fusion | flops 810024960 | bytes 2998272 | tf_op jit(solution)/shard_map/jvp(ghcij,cjghp->cighp)/dot_general | solution.py:63
  164.4 3.7 %fusion.28 = f32[1,256,1,16,64]{1,4,3,2,0:T(8,128)} fusion(bf16[16,64,256]{2,1,0:T(8,128)(2,1)S(1)} %bitcast.282, f32[16,256]{1,0:T(8,128)S(1)} %bitcast.298, f32[16,256]{1,0:T(8,128)S(1)} %copy-done.21, f32[256,256]{1,0:T(8,128)S(1)} %copy-done.9, pred[256,256]{1,0:T(8,128)(4,1)S(1)} %copy-done.18, f32[256,16,64]{0,2,1:T(8,128)S(1)} %copy-done.3, ...), kind=kOutput, calls=%fused_computation.33 | convolution fusion | flops 810024960 | bytes 2998272 | tf_op jit(solution)/shard_map/transpose(jvp(ghcij,cjghp->cighp))/dot_general | solution.py:63
  168.1 0.8 pad_maximum_fusion.1
  168.9 6.7 %all-to-all-start = ((f32[16,32,128]{2,1,0:T(8,128)}), f32[16,32,128]{2,1,0:T(8,128)S(1)}, u32[]{:S(2)}, u32[]{:S(2)}) async-start(f32[16,32,128]{2,1,0:T(8,128)} %pad_maximum_fusion.1), calls=%async_computation | async-start | bytes 524288 | tf_op jit(solution)/shard_map/all_to_all | solution.py:36
  175.6 1.9 fusion.40
  177.7 1.0 copy.241
  178.9 0.7 copy.242
  179.5 1.0 copy.240
  180.5 2.7 %all-to-all-done = f32[16,32,128]{2,1,0:T(8,128)S(1)} async-done(((f32[16,32,128]{2,1,0:T(8,128)}), f32[16,32,128]{2,1,0:T(8,128)S(1)}, u32[]{:S(2)}, u32[]{:S(2)}) %all-to-all-start) | async-done | bytes 262176 | tf_op jit(solution)/shard_map/all_to_all | solution.py:36
  183.3 0.2 fusion.36
  183.5 0.2 fusion.35
  183.7 0.6 convert_element_type.108
  184.3 0.6 convert_element_type.111
  (105 shorter events, 2.4 us)
Async XLA Ops:
  7.2 7.2 %copy-start.10 = (f32[1,16,256]{2,1,0:T(8,128)S(1)}, f32[1,16,256]{2,1,0:T(8,128)}, u32[]{:S(2)}) copy-start(f32[1,16,256]{2,1,0:T(8,128)} %param.10) | copy-start | bytes 49156
  7.2 7.9 %copy-start.5 = (bf16[1,256,1024]{2,1,0:T(8,128)(2,1)S(1)}, bf16[1,256,1024]{2,1,0:T(8,128)(2,1)}, u32[]{:S(2)}) copy-start(bf16[1,256,1024]{2,1,0:T(8,128)(2,1)} %param.9) | copy-start | bytes 1572868
  7.2 8.1 %copy-start.6 = (bf16[1,256,1024]{2,1,0:T(8,128)(2,1)S(1)}, bf16[1,256,1024]{2,1,0:T(8,128)(2,1)}, u32[]{:S(2)}) copy-start(bf16[1,256,1024]{2,1,0:T(8,128)(2,1)} %param.13) | copy-start | bytes 1572868
  7.2 67.2 %all-gather.7.cloned.1.call-start = ((), (), s32[]{:S(2)}) async-start(), calls=%async_computation.2 | async-start | bytes 8912896 | tf_op jit(solution)/shard_map/all_gather | solution.py:125
  8.0 0.8 copy-start.22
  8.8 3.6 %copy-start.1 = (f32[1,16,256]{1,2,0:T(8,128)}, f32[1,16,256]{1,2,0:T(8,128)S(1)}, u32[]{:S(2)}) copy-start(f32[1,16,256]{1,2,0:T(8,128)S(1)} %copy.208) | copy-start | bytes 49156
  12.6 5.4 %copy-start = (s32[16]{0:T(128)S(1)}, s32[16]{0:T(128)}, u32[]{:S(2)}) copy-start(s32[16]{0:T(128)} %param.16) | copy-start | bytes 196
  14.0 13.0 %copy-start.25 = (f32[16]{0:T(128)S(1)}, f32[16]{0:T(128)}, u32[]{:S(2)}) copy-start(f32[16]{0:T(128)} %param.12) | copy-start | bytes 196
  14.0 117.3 %all-gather.5.cloned.1.call-start = ((), (), s32[]{:S(2)}) async-start(), calls=%async_computation.1 | async-start | bytes 9052160 | tf_op jit(solution)/shard_map/all_gather | solution.py:20
  131.3 3.4 %slice-start = ((f32[16,1,16,8193]{3,2,1,0:T(8,128)}), f32[16,1,16,8192]{3,2,1,0:T(8,128)S(1)}, s32[]{:S(2)}) async-start(f32[16,1,16,8193]{3,2,1,0:T(8,128)} %all-gather.5.cloned.1.call-done), calls=%async_computation.3 | async-start | bytes 16777216 | tf_op jit(solution)/shard_map/slice | solution.py:22
  134.7 1.7 slice-start.1
  134.7 2.3 %copy-start.11 = (f32[1,16,256]{2,1,0:T(8,128)S(1)}, f32[1,16,256]{2,1,0:T(8,128)}, u32[]{:S(2)}) copy-start(f32[1,16,256]{2,1,0:T(8,128)} %param.10) | copy-start | bytes 49156
  134.7 2.3 %copy-start.15 = (f32[16,256]{1,0:T(8,128)S(1)}, f32[16,256]{1,0:T(8,128)}, u32[]{:S(2)}) copy-start(f32[16,256]{1,0:T(8,128)} %copy.252) | copy-start | bytes 49156
  134.7 2.3 %copy-start.16 = (f32[1,16,1,2,128]{4,3,1,2,0:T(2,128)S(1)}, f32[1,16,1,2,128]{4,3,1,2,0:T(2,128)}, u32[]{:S(2)}) copy-start(f32[1,16,1,2,128]{4,3,1,2,0:T(2,128)} %copy.210) | copy-start | bytes 49156
  136.3 1.9 copy-start.8
  136.3 1.8 copy-start.17
  137.1 4.7 %copy-start.13 = (f32[256,16]{0,1:T(8,128)}, f32[256,16]{0,1:T(8,128)S(1)}, u32[]{:S(2)}) copy-start(f32[256,16]{0,1:T(8,128)S(1)} %get-tuple-element.50) | copy-start | bytes 49156
  137.1 4.7 %copy-start.20 = (f32[16,256]{1,0:T(8,128)}, f32[16,256]{1,0:T(8,128)S(1)}, u32[]{:S(2)}) copy-start(f32[16,256]{1,0:T(8,128)S(1)} %get-tuple-element.51) | copy-start | bytes 49156
  138.2 9.1 %copy-start.2 = (f32[1,16,256]{1,2,0:T(8,128)S(1)}, f32[1,16,256]{1,2,0:T(8,128)}, u32[]{:S(2)}) copy-start(f32[1,16,256]{1,2,0:T(8,128)} %copy-done.1) | copy-start | bytes 49156
  141.8 9.1 %copy-start.4 = (f32[1,16,256]{1,2,0:T(8,128)S(1)}, f32[1,16,256]{1,2,0:T(8,128)}, u32[]{:S(2)}) copy-start(f32[1,16,256]{1,2,0:T(8,128)} %copy.219) | copy-start | bytes 49156
  158.5 5.9 %copy-start.3 = (f32[256,16,64]{0,2,1:T(8,128)S(1)}, f32[256,16,64]{0,2,1:T(8,128)}, u32[]{:S(2)}) copy-start(f32[256,16,64]{0,2,1:T(8,128)} %get-tuple-element.63) | copy-start | bytes 3145732
  158.5 5.9 %copy-start.9 = (f32[256,256]{1,0:T(8,128)S(1)}, f32[256,256]{1,0:T(8,128)}, u32[]{:S(2)}) copy-start(f32[256,256]{1,0:T(8,128)} %fusion.78) | copy-start | bytes 786436
  158.5 5.9 %copy-start.12 = (f32[1,16,256]{2,1,0:T(8,128)S(1)}, f32[1,16,256]{2,1,0:T(8,128)}, u32[]{:S(2)}) copy-start(f32[1,16,256]{2,1,0:T(8,128)} %param.10) | copy-start | bytes 49156
  158.5 5.9 %copy-start.14 = (f32[256,16]{0,1:T(8,128)S(1)}, f32[256,16]{0,1:T(8,128)}, u32[]{:S(2)}) copy-start(f32[256,16]{0,1:T(8,128)} %copy-done.13) | copy-start | bytes 49156
  158.5 5.9 %copy-start.18 = (pred[256,256]{1,0:T(8,128)(4,1)S(1)}, pred[256,256]{1,0:T(8,128)(4,1)}, u32[]{:S(2)}) copy-start(pred[256,256]{1,0:T(8,128)(4,1)} %iota_compare_fusion) | copy-start | bytes 196612
  158.5 5.9 %copy-start.21 = (f32[16,256]{1,0:T(8,128)S(1)}, f32[16,256]{1,0:T(8,128)}, u32[]{:S(2)}) copy-start(f32[16,256]{1,0:T(8,128)} %copy-done.20) | copy-start | bytes 49156
  164.4 3.8 %copy-start.7 = (f32[1,256,1,128]{3,1,2,0:T(8,128)S(1)}, f32[1,256,1,128]{3,1,2,0:T(8,128)}, u32[]{:S(2)}) copy-start(f32[1,256,1,128]{3,1,2,0:T(8,128)} %copy.237) | copy-start | bytes 393220
  168.1 9.4 %copy-start.19 = (f32[16,256]{1,0:T(8,128)S(1)}, f32[16,256]{1,0:T(8,128)}, u32[]{:S(2)}) copy-start(f32[16,256]{1,0:T(8,128)} %get-tuple-element.42) | copy-start | bytes 49156
  168.1 10.7 %copy-start.23 = (f32[16]{0:T(128)S(1)}, f32[16]{0:T(128)}, u32[]{:S(2)}) copy-start(f32[16]{0:T(128)} %copy-done.22) | copy-start | bytes 196
  168.9 14.4 %copy-start.24 = (s32[16]{0:T(128)S(1)}, s32[16]{0:T(128)}, u32[]{:S(2)}) copy-start(s32[16]{0:T(128)} %and_select_fusion) | copy-start | bytes 196
  168.9 14.3 %all-to-all-start = ((f32[16,32,128]{2,1,0:T(8,128)}), f32[16,32,128]{2,1,0:T(8,128)S(1)}, u32[]{:S(2)}, u32[]{:S(2)}) async-start(f32[16,32,128]{2,1,0:T(8,128)} %pad_maximum_fusion.1), calls=%async_computation | async-start | bytes 524288 | tf_op jit(solution)/shard_map/all_to_all | solution.py:36
Sparse Core Ops, SparseCore 0:
  14.1 60.1 all-gather.6
  76.2 55.0 all-gather.4
where the time goes:
time: 193 us; the launch traced here: 192 us
  waiting for transfers between devices  66.1 us (34%)
  matrix products  37 us (19%)
  local copies, waits for them, and re-layouts  27.4 us (14%)
  blocking collectives  21.2 us (11%)
  between operations  19.9 us (10%)
  other arithmetic  13.5 us (7%)
  starting transfers between devices  6.74 us (3%)
    all_gather x1, waiting for transfers between devices, sent_together(): result, at, done = (lax.all_gather(both, axis, axis=dim, tiled=True), 0, [])  42.7 us
    all_gather x1, blocking collectives, shards(): lax.all_gather(decay_all[None], 'seg', axis=0, tiled=True)  21.2 us
    all_gather x1, waiting for transfers between devices, shards(): lax.all_gather(start_part[None], 'seg', axis=0, tiled=True)  20.7 us
    dot_general x3, matrix products, ssd_forward(): jnp.einsum('ghcij,cjghp->cighp', weights, value_blk, precision=exact_mode)  13.1 us
    dot_general x1, matrix products, shards(): jnp.einsum('dgh,dghpn->ghpn', factors, gathered_part, precision=exact_mode)  12.5 us
    unnamed x64, local copies, waits for them, and re-layouts  8.56 us
    all_to_all x1, starting transfers between devices, sent_together_2(): lax.all_to_all(both, axis, split_axis=split_dim, concat_axis=concat_dim,...  6.66 us
    another operation x8, other arithmetic  4 us
  transfers between devices with their start and end apart: 3, of which 3 were waited for; matrix products, arithmetic and copies ran while one was open for 17% of the time, Pallas kernels for 0%

commit v1 on v0

v1 whole, which is shorter than its diff:
```python
import functools

import jax
import jax.numpy as jnp
from jax import lax
from jax.experimental import pallas as pl
from jax.experimental.pallas import tpu as pltpu
from jax.sharding import PartitionSpec as P

P_SIZE = 64
N = 128
HEADS_PER_GROUP = 32
LENGTH = 256
SEGS = 16
KIDS = 4
F32, BF16 = jnp.float32, jnp.bfloat16
MESH = pl.DeviceIdType.MESH


def dot_nn(a, b):
    return lax.dot_general(a, b, (((1,), (0,)), ((), ())), preferred_element_type=F32)


def dot_nt(a, b):
    return lax.dot_general(a, b, (((1,), (1,)), ((), ())), preferred_element_type=F32)


def dot_tn(a, b):
    return lax.dot_general(a, b, (((0,), (0,)), ((), ())), preferred_element_type=F32)


def halves(v):
    high = v.astype(BF16)
    return high, (v - high.astype(F32)).astype(BF16)


def thirds(v):
    high, rest = v.astype(BF16), v
    rest = v - high.astype(F32)
    mid = rest.astype(BF16)
    return high, mid, (rest - mid.astype(F32)).astype(BF16)


def sum_with(v, ones):
    high, mid, low = thirds(v)
    return dot_nn(high, ones) + (dot_nn(mid, ones) + dot_nn(low, ones))


def kernel(
    heads, owners, wide,
    parents, rates, skips, deltas_hbm, x_hbm, dy_hbm, b_hbm, c_hbm,
    out_hbm, gx_hbm, gd_hbm, gw_hbm, gr_hbm,
    deltas, x, dy, b, c, xh, xl, yh, yl, x2, y2, e1x, e2x, y_in, h_in,
    u_buf, v_buf, a_buf, u_got, v_got, a_got, e_one, s_buf, e_buf, s_all, e_all,
    dc_buf, db_buf, dc_got, db_got, out_v, gx_v, gd_v, gw_v, gr_v, kids, pidx, gidx,
    in_sem, out_sem, su, ru, sv, rv, sa, ra, ss, rs, se, re, sc, rc, sb, rb,
):
    columns = heads * P_SIZE
    rows = LENGTH // owners
    half = N // 2
    seg, head = lax.axis_index("seg"), lax.axis_index("head")
    my_z, my_core = seg // 2, lax.rem(seg, 2)
    group_col = pl.multiple_of((head * heads // HEADS_PER_GROUP) * N, N)

    def load(src, dst, k):
        return pltpu.make_async_copy(src, dst, in_sem.at[k])

    loads = [
        load(deltas_hbm.at[0], deltas, 0),
        load(b_hbm.at[0, :, pl.ds(group_col, N)], b, 1),
        load(x_hbm.at[0], x, 2),
        load(c_hbm.at[0, :, pl.ds(group_col, N)], c, 3),
        load(dy_hbm.at[0], dy, 4),
    ]
    for one in loads:
        one.start()

    barrier = pltpu.get_barrier_semaphore()

    def greet_seg(d, carry):
        pl.semaphore_signal(barrier, inc=1, device_id=(lax.rem(seg + d, SEGS), head), device_id_type=MESH)
        return carry

    def greet_head(d, carry):
        pl.semaphore_signal(barrier, inc=1, device_id=(seg, lax.rem(head + d, owners)), device_id_type=MESH)
        return carry

    lax.fori_loop(1, SEGS, greet_seg, 0)
    lax.fori_loop(1, owners, greet_head, 0)

    def table(s, carry):
        c0 = c1 = c2 = c3 = jnp.int32(SEGS)
        for k in range(SEGS - 1, -1, -1):
            hit = parents[k] == s
            c3 = jnp.where(hit, c2, c3)
            c2 = jnp.where(hit, c1, c2)
            c1 = jnp.where(hit, c0, c1)
            c0 = jnp.where(hit, k, c0)
        kids[KIDS * s] = c0
        kids[KIDS * s + 1] = c1
        kids[KIDS * s + 2] = c2
        kids[KIDS * s + 3] = c3
        p = parents[s]
        g = parents[jnp.maximum(p, 0)]
        pidx[s] = jnp.where(p < 0, SEGS, p)
        gidx[s] = jnp.where(p < 0, SEGS, jnp.where(g < 0, SEGS, g))
        return carry

    u_got[SEGS] = jnp.zeros((half, N), BF16)
    v_got[SEGS] = jnp.zeros((half, N), BF16)
    a_got[SEGS] = jnp.zeros((1, N), F32)
    e_one[SEGS] = jnp.zeros((half, N), F32)

    row_h = lax.broadcasted_iota(jnp.int32, (heads, 1), 0)
    rate_col = jnp.zeros((heads, 1), F32)
    for h in range(heads):
        rate_col = jnp.where(row_h == h, rates[h], rate_col)

    t_row = lax.broadcasted_iota(jnp.int32, (LENGTH, LENGTH), 0)
    t_col = lax.broadcasted_iota(jnp.int32, (LENGTH, LENGTH), 1)
    upto = (t_row <= t_col).astype(BF16)
    causal = t_row >= t_col

    pick_row = lax.rem(lax.broadcasted_iota(jnp.int32, (2 * heads, columns), 0), heads)
    pick_col = lax.broadcasted_iota(jnp.int32, (2 * heads, columns), 1) // P_SIZE
    pick2 = (pick_row == pick_col).astype(BF16)
    pick1 = pick2[:heads]

    loads[0].wait()
    delta = deltas[...]
    run = sum_with(-rate_col * delta, upto)
    mid = run[:, LENGTH - 1 :] * 0.5
    e1 = jnp.exp(run - mid)
    e2 = jnp.exp(mid - run) * delta
    emid = jnp.broadcast_to(jnp.exp(mid), (heads, 8))
    e1s = jnp.concatenate(halves(e1), axis=0)
    e2s = jnp.concatenate(halves(e2), axis=0)
    ems = jnp.concatenate(halves(emid), axis=0)
    em_row = dot_tn(ems, pick2)[:1]

    blocks = [slice(k, k + wide) for k in range(0, columns, wide)]

    loads[1].wait()
    loads[2].wait()
    bt = b[...].T
    for cut in blocks:
        ex = dot_tn(e2s, pick2[:, cut])
        e2x[:, cut] = ex
        scaled = ex * x[:, cut].astype(F32)
        high, low = halves(scaled)
        xh[:, cut] = high
        xl[:, cut] = low
        u_buf[:, cut] = (em_row[:, cut] * (dot_nn(bt, high) + dot_nn(bt, low))).astype(BF16)
    for z in range(SEGS // 2):
        part = em_row[:, z * N : (z + 1) * N]
        a_buf[z] = part * part

    pl.semaphore_wait(barrier, SEGS - 1 + owners - 1)

    def seg_peer(d):
        peer = lax.rem(seg + d, SEGS)
        came = lax.rem(seg - d + SEGS, SEGS)
        return peer, came

    def spot(ref, s):
        z, core = s // 2, lax.rem(s, 2)
        return ref.at[pl.ds(pl.multiple_of(core * half, half), half), pl.ds(pl.multiple_of(z * N, N), N)]

    def up_copy(buf, got, send, recv, d, dst):
        peer, _ = seg_peer(d)
        return pltpu.make_async_remote_copy(
            src_ref=spot(buf, peer), dst_ref=got.at[dst], send_sem=send.at[d], recv_sem=recv.at[d],
            device_id=(peer, head), device_id_type=MESH,
        )

    def a_copy(d, dst):
        peer, _ = seg_peer(d)
        return pltpu.make_async_remote_copy(
            src_ref=a_buf.at[peer // 2], dst_ref=a_got.at[dst], send_sem=sa.at[d], recv_sem=ra.at[d],
            device_id=(peer, head), device_id_type=MESH,
        )

    def down_copy(buf, whole, send, recv, d, owner):
        peer, _ = seg_peer(d)
        return pltpu.make_async_remote_copy(
            src_ref=buf.at[peer], dst_ref=spot(whole, owner), send_sem=send.at[d], recv_sem=recv.at[d],
            device_id=(peer, head), device_id_type=MESH,
        )

    def send_u(d, carry):
        up_copy(u_buf, u_got, su, ru, d, seg).start()
        a_copy(d, seg).start()
        return carry

    lax.fori_loop(1, SEGS, send_u, 0)
    u_got[seg] = spot(u_buf, seg)[...]
    a_got[seg] = a_buf[my_z]

    loads[3].wait()
    loads[4].wait()
    ct = c[...].T
    for cut in blocks:
        ex = dot_tn(e1s, pick2[:, cut])
        e1x[:, cut] = ex
        scaled = ex * dy[:, cut].astype(F32)
        high, low = halves(scaled)
        yh[:, cut] = high
        yl[:, cut] = low
        v_buf[:, cut] = (em_row[:, cut] * (dot_nn(ct, high) + dot_nn(ct, low))).astype(BF16)

    def send_v(d, carry):
        up_copy(v_buf, v_got, sv, rv, d, seg).start()
        return carry

    lax.fori_loop(1, SEGS, send_v, 0)
    v_got[seg] = spot(v_buf, seg)[...]

    lax.fori_loop(0, SEGS, table, 0)
    gram = jnp.where(causal, dot_nt(c[...], b[...]), 0.0)
    gram_t = jnp.where(t_row <= t_col, dot_nt(b[...], c[...]), 0.0)
    gh, gl = halves(gram)
    th, tl = halves(gram_t)
    k_sum = jnp.zeros((LENGTH, LENGTH), F32)
    for cut in blocks:
        x_high, x_low, y_high, y_low = xh[:, cut], xl[:, cut], yh[:, cut], yl[:, cut]
        y_in[:, cut] = e1x[:, cut] * (dot_nn(gh, x_high) + (dot_nn(gh, x_low) + dot_nn(gl, x_high)))
        h_in[:, cut] = e2x[:, cut] * (dot_nn(th, y_high) + (dot_nn(th, y_low) + dot_nn(tl, y_high)))
        k_sum += dot_nt(y_high, x_high) + (dot_nt(y_high, x_low) + dot_nt(y_low, x_high))
        e1x[:, cut] = e1x[:, cut] * em_row[:, cut]
        e2x[:, cut] = e2x[:, cut] * em_row[:, cut]
        x2[:, cut] = (e2x[:, cut] * x[:, cut].astype(F32)).astype(BF16)
        y2[:, cut] = (e1x[:, cut] * dy[:, cut].astype(F32)).astype(BF16)
    k_sum = jnp.where(causal, k_sum, 0.0)
    kh, kl = halves(k_sum)
    dc_buf[...] = dot_nn(kh, b[...]) + dot_nn(kl, b[...])
    db_buf[...] = dot_tn(kh, c[...]) + dot_tn(kl, c[...])

    def wait_u(d, carry):
        _, came = seg_peer(d)
        up_copy(u_buf, u_got, su, ru, d, came).wait_recv()
        a_copy(d, came).wait_recv()
        return carry

    lax.fori_loop(1, SEGS, wait_u, 0)

    def start_of(s):
        p, g = pidx[s], gidx[s]
        s_buf[s] = (a_got[p] * u_got[g].astype(F32) + u_got[p].astype(F32)).astype(BF16)

    def send_s(d, carry):
        peer, _ = seg_peer(d)
        start_of(peer)
        down_copy(s_buf, s_all, ss, rs, d, seg).start()
        return carry

    lax.fori_loop(1, SEGS, send_s, 0)
    start_of(seg)
    spot(s_all, seg)[...] = s_buf[seg]

    def wait_v(d, carry):
        _, came = seg_peer(d)
        up_copy(v_buf, v_got, sv, rv, d, came).wait_recv()
        return carry

    lax.fori_loop(1, SEGS, wait_v, 0)

    def first_e(s, carry):
        total = v_got[kids[KIDS * s]].astype(F32)
        for k in range(1, KIDS):
            total += v_got[kids[KIDS * s + k]].astype(F32)
        e_one[s] = total
        return carry

    lax.fori_loop(0, SEGS, first_e, 0)

    def end_grad(s):
        total = e_one[s]
        for k in range(KIDS):
            kid = kids[KIDS * s + k]
            total += a_got[kid] * e_one[kid]
        e_buf[s] = total.astype(BF16)

    def send_e(d, carry):
        peer, _ = seg_peer(d)
        end_grad(peer)
        down_copy(e_buf, e_all, se, re, d, seg).start()
        return carry

    lax.fori_loop(1, SEGS, send_e, 0)
    end_grad(seg)
    spot(e_all, seg)[...] = e_buf[seg]

    def head_copy(buf, got, send, recv, d, dst):
        peer = lax.rem(head + d, owners)
        return pltpu.make_async_remote_copy(
            src_ref=buf.at[pl.ds(pl.multiple_of(peer * rows, rows), rows)], dst_ref=got.at[dst],
            send_sem=send.at[d], recv_sem=recv.at[d], device_id=(seg, peer), device_id_type=MESH,
        )

    def skip_row(at):
        lane = lax.broadcasted_iota(jnp.int32, (1, wide), 1) // P_SIZE
        row = jnp.zeros((1, wide), F32)
        for h in range(wide // P_SIZE):
            row = jnp.where(lane == h, skips[at // P_SIZE + h], row)
        return row

    def wait_s(d, carry):
        _, came = seg_peer(d)
        down_copy(s_buf, s_all, ss, rs, d, came).wait_recv()
        return carry

    lax.fori_loop(1, SEGS, wait_s, 0)
    d_one = jnp.zeros((heads, LENGTH), F32)
    dc = dc_buf[...]
    for cut in blocks:
        core = y_in[:, cut] + e1x[:, cut] * dot_nn(c[...], s_all[:, cut])
        out_v[:, cut] = (core + skip_row(cut.start) * x[:, cut].astype(F32)).astype(BF16)
        high, low = halves(core * dy[:, cut].astype(F32))
        d_one += dot_nt(pick1[:, cut], high) + dot_nt(pick1[:, cut], low)
        dc += dot_nt(y2[:, cut], s_all[:, cut])
    dc_buf[...] = dc
    out_copy = pltpu.make_async_copy(out_v, out_hbm.at[0], out_sem.at[0])
    out_copy.start()

    def send_dc(d, carry):
        head_copy(dc_buf, dc_got, sc, rc, d, head).start()
        return carry

    lax.fori_loop(1, owners, send_dc, 0)
    dc_got[head] = dc_buf[pl.ds(pl.multiple_of(head * rows, rows), rows)]

    def wait_e(d, carry):
        _, came = seg_peer(d)
        down_copy(e_buf, e_all, se, re, d, came).wait_recv()
        return carry

    lax.fori_loop(1, SEGS, wait_e, 0)
    d_two = jnp.zeros((heads, LENGTH), F32)
    d_last = jnp.zeros((heads, 8), F32)
    db = db_buf[...]
    for cut in blocks:
        ends = e_all[:, cut]
        x_cut = x[:, cut].astype(F32)
        late = e2x[:, cut] * dot_nn(b[...], ends)
        grad = h_in[:, cut] + late
        gx_v[:, cut] = (grad + skip_row(cut.start) * dy[:, cut].astype(F32)).astype(BF16)
        high, low = halves(grad * x_cut)
        d_two += dot_nt(pick1[:, cut], high) + dot_nt(pick1[:, cut], low)
        em = em_row[:, cut]
        both = jnp.sum(ends.astype(F32) * s_all[:, cut].astype(F32), axis=0, keepdims=True)
        tail = jnp.sum(late * x_cut, axis=0, keepdims=True) + em * em * both
        high, low = halves(jnp.broadcast_to(tail, (8, wide)))
        d_last += dot_nt(pick1[:, cut], high) + dot_nt(pick1[:, cut], low)
        db += dot_nt(x2[:, cut], ends)
    db_buf[...] = db

    def send_db(d, carry):
        head_copy(db_buf, db_got, sb, rb, d, head).start()
        return carry

    lax.fori_loop(1, owners, send_db, 0)
    db_got[head] = db_buf[pl.ds(pl.multiple_of(head * rows, rows), rows)]
    gx_copy = pltpu.make_async_copy(gx_v, gx_hbm.at[0], out_sem.at[1])
    gx_copy.start()

    since = (t_row >= t_col).astype(BF16)
    later = sum_with(d_one - d_two, since) + d_last[:, :1]
    gd_v[...] = d_two / delta - rate_col * later
    gd_copy = pltpu.make_async_copy(gd_v, gd_hbm.at[0], out_sem.at[2])
    gd_copy.start()

    share = max(1, HEADS_PER_GROUP // heads)

    def finish(got, buf, send, recv, dst):
        def wait_one(d, carry):
            head_copy(buf, got, send, recv, d, lax.rem(head - d + owners, owners)).wait_recv()
            return carry

        lax.fori_loop(1, owners, wait_one, 0)
        for g in range(owners // share):
            total = got[g * share]
            for k in range(1, share):
                total += got[g * share + k]
            dst[:, g * N : (g + 1) * N] = total.astype(BF16)

    finish(dc_got, dc_buf, sc, rc, gr_v)
    gr_copy = pltpu.make_async_copy(gr_v, gr_hbm.at[0], out_sem.at[3])
    gr_copy.start()
    finish(db_got, db_buf, sb, rb, gw_v)
    gw_copy = pltpu.make_async_copy(gw_v, gw_hbm.at[0], out_sem.at[4])
    gw_copy.start()

    def drain_seg(d, carry):
        up_copy(u_buf, u_got, su, ru, d, seg).wait_send()
        a_copy(d, seg).wait_send()
        up_copy(v_buf, v_got, sv, rv, d, seg).wait_send()
        down_copy(s_buf, s_all, ss, rs, d, seg).wait_send()
        down_copy(e_buf, e_all, se, re, d, seg).wait_send()
        return carry

    def drain_head(d, carry):
        head_copy(dc_buf, dc_got, sc, rc, d, head).wait_send()
        head_copy(db_buf, db_got, sb, rb, d, head).wait_send()
        return carry

    lax.fori_loop(1, SEGS, drain_seg, 0)
    lax.fori_loop(1, owners, drain_head, 0)
    for one in (out_copy, gx_copy, gd_copy, gr_copy, gw_copy):
        one.wait()


def shards(owners, inputs, deltas, rates, skips, writer, reader, grad_out, parents, levels):
    heads = deltas.shape[1]
    columns = inputs.shape[2]
    rows = LENGTH // owners
    half = N // 2
    vm = pltpu.VMEM
    wide_b = lambda: vm((LENGTH, columns), BF16)
    wide_f = lambda: vm((LENGTH, columns), F32)
    sem = lambda n: pltpu.SemaphoreType.DMA((n,))
    anywhere = pl.BlockSpec(memory_space=pl.ANY)
    scalars = pl.BlockSpec(memory_space=pltpu.SMEM)
    return tuple(
        pl.pallas_call(
            functools.partial(kernel, heads, owners, 256),
            out_shape=(
                jax.ShapeDtypeStruct(inputs.shape, BF16),
                jax.ShapeDtypeStruct(inputs.shape, BF16),
                jax.ShapeDtypeStruct(deltas.shape, F32),
                jax.ShapeDtypeStruct((1, rows, writer.shape[2]), BF16),
                jax.ShapeDtypeStruct((1, rows, writer.shape[2]), BF16),
            ),
            in_specs=[scalars] * 3 + [anywhere] * 5,
            out_specs=[anywhere] * 5,
            scratch_shapes=[
                vm((heads, LENGTH), F32), wide_b(), wide_b(), vm((LENGTH, N), BF16), vm((LENGTH, N), BF16),
                wide_b(), wide_b(), wide_b(), wide_b(), wide_b(), wide_b(), wide_f(), wide_f(), wide_f(), wide_f(),
                vm((N, columns), BF16), vm((N, columns), BF16), vm((SEGS // 2, 1, N), F32),
                vm((SEGS + 1, half, N), BF16), vm((SEGS + 1, half, N), BF16), vm((SEGS + 1, 1, N), F32),
                vm((SEGS + 1, half, N), F32), vm((SEGS, half, N), BF16), vm((SEGS, half, N), BF16),
                vm((N, columns), BF16), vm((N, columns), BF16),
                vm((LENGTH, N), F32), vm((LENGTH, N), F32), vm((owners, rows, N), F32), vm((owners, rows, N), F32),
                wide_b(), wide_b(), vm((heads, LENGTH), F32),
                vm((rows, writer.shape[2]), BF16), vm((rows, writer.shape[2]), BF16),
                pltpu.SMEM((KIDS * SEGS,), jnp.int32), pltpu.SMEM((SEGS,), jnp.int32), pltpu.SMEM((SEGS,), jnp.int32),
                sem(5), sem(5),
            ] + [sem(SEGS)] * 10 + [sem(owners)] * 4,
            compiler_params=pltpu.CompilerParams(
                collective_id=0, has_side_effects=True, vmem_limit_bytes=48 * 1024 * 1024
            ),
            name="tree_scan",
        )(parents, rates, skips, deltas, inputs, grad_out, writer, reader)
    )


def solution(mesh):
    placed = (
        P("seg", None, "head"),
        P("seg", "head", None),
        P("head"),
        P("head"),
        P("seg", None, None),
        P("seg", None, None),
        P("seg", None, "head"),
        P(),
        P(),
    )
    return jax.shard_map(
        functools.partial(shards, mesh.shape["head"]),
        mesh=mesh,
        in_specs=placed,
        out_specs=(
            P("seg", None, "head"),
            P("seg", None, "head"),
            P("seg", "head", None),
            P("seg", "head", None),
            P("seg", "head", None),
        ),
        check_vma=False,
    )
```

time: 193 us -> 55.7 us (0.29)
  waiting for transfers between devices: 66.1 us -> 0 us
  Pallas kernels: 0 us -> 44.4 us
  matrix products: 37 us -> 0 us
  blocking collectives: 21.2 us -> 0 us
  between operations: 19.9 us -> 0.66 us
  local copies, waits for them, and re-layouts: 27.4 us -> 10.3 us
  other arithmetic: 13.5 us -> 0 us
  starting transfers between devices: 6.74 us -> 0 us
    all_gather x2 -> x0, waiting for transfers between devices: 63.4 us -> none  [the longest x1 42.7 us: sent_together(): result, at, done = (lax.all_gather(both, axis, axis=dim, tiled=True), 0, [])]
    pallas_call x0 -> x1, Pallas kernels: none -> 44.4 us  [shards(): pl.pallas_call(functools.partial(kernel, heads, owners, 256), out_shape=(...]
    dot_general x15 -> x0, matrix products: 37 us -> none  [the longest x3 13.1 us: ssd_forward(): jnp.einsum('ghcij,cjghp->cighp', weights, value_blk, precision=exact_mode)]
    all_gather x1 -> x0, blocking collectives: 21.2 us -> none  [shards(): lax.all_gather(decay_all[None], 'seg', axis=0, tiled=True)]
    all_to_all x1 -> x0, starting transfers between devices: 6.66 us -> none  [sent_together_2(): lax.all_to_all(both, axis, split_axis=split_dim, concat_axis=concat_dim,...]
    another operation x8 -> x0, other arithmetic: 4 us -> none
    another operation x21 -> x0, local copies, waits for them, and re-layouts: 3.88 us -> none
    slice x6 -> x0, local copies, waits for them, and re-layouts: 3.82 us -> none  [the longest x4 3.38 us: sent_together(): piece = result[..., at:at + column.shape[along]]]
  transfers between devices with their start and end apart: 3 -> 0, of which waited for: 3 -> 0; matrix products, arithmetic and copies ran while one was open for 17% -> 0% of each run, Pallas kernels for 0% -> 0%
where the time goes in v1:
time: 55.7 us; the launch traced here: 55.4 us
  Pallas kernels  44.4 us (80%)
  local copies, waits for them, and re-layouts  10.3 us (18%)
  between operations  0.66 us (1%)
    pallas_call x1, Pallas kernels, shards(): pl.pallas_call(functools.partial(kernel, heads, owners, 256), out_shape=(...  44.4 us
    unnamed x21, local copies, waits for them, and re-layouts  10.3 us

profile of v1, /device:TPU:1, one launch (start us, length us, event | category | flops | bytes accessed | tf_op | source)
XLA Modules:
  0.0 55.4 jit_solution(17930681373448628910)
XLA Ops:
  0.6 0.0 copy-start
  0.6 1.0 %copy-done = bf16[1,256,1024]{2,1,0:T(8,128)(2,1)S(1)} copy-done((bf16[1,256,1024]{2,1,0:T(8,128)(2,1)S(1)}, bf16[1,256,1024]{2,1,0:T(8,128)(2,1)}, u32[]{:S(2)}) %copy-start) | copy-done | bytes 524312
  1.7 0.0 copy-start.1
  1.7 1.0 %copy-done.1 = bf16[1,256,1024]{2,1,0:T(8,128)(2,1)S(1)} copy-done((bf16[1,256,1024]{2,1,0:T(8,128)(2,1)S(1)}, bf16[1,256,1024]{2,1,0:T(8,128)(2,1)}, u32[]{:S(2)}) %copy-start.1) | copy-done | bytes 524312
  2.7 0.0 copy-start.2
  2.7 1.0 %copy-done.2 = bf16[1,256,1024]{2,1,0:T(8,128)(2,1)S(1)} copy-done((bf16[1,256,1024]{2,1,0:T(8,128)(2,1)S(1)}, bf16[1,256,1024]{2,1,0:T(8,128)(2,1)}, u32[]{:S(2)}) %copy-start.2) | copy-done | bytes 524312
  3.8 0.0 copy-start.3
  3.8 1.0 %copy-done.3 = bf16[1,256,1024]{2,1,0:T(8,128)(2,1)S(1)} copy-done((bf16[1,256,1024]{2,1,0:T(8,128)(2,1)S(1)}, bf16[1,256,1024]{2,1,0:T(8,128)(2,1)}, u32[]{:S(2)}) %copy-start.3) | copy-done | bytes 524312
  4.8 0.0 copy-start.4
  4.8 0.7 %copy-done.4 = f32[1,16,256]{2,1,0:T(8,128)S(1)} copy-done((f32[1,16,256]{2,1,0:T(8,128)S(1)}, f32[1,16,256]{2,1,0:T(8,128)}, u32[]{:S(2)}) %copy-start.4) | copy-done | bytes 16408
  5.5 0.0 copy-start.5
  5.5 0.7 %copy-done.5 = s32[16]{0:T(128)S(1)} copy-done((s32[16]{0:T(128)S(1)}, s32[16]{0:T(128)}, u32[]{:S(2)}) %copy-start.5) | copy-done | bytes 88
  6.2 0.0 copy-start.6
  6.2 0.7 %copy-done.6 = f32[16]{0:T(128)S(1)} copy-done((f32[16]{0:T(128)S(1)}, f32[16]{0:T(128)}, u32[]{:S(2)}) %copy-start.6) | copy-done | bytes 88
  6.8 0.0 copy-start.7
  6.8 0.7 %copy-done.7 = f32[16]{0:T(128)S(1)} copy-done((f32[16]{0:T(128)S(1)}, f32[16]{0:T(128)}, u32[]{:S(2)}) %copy-start.7) | copy-done | bytes 88
  7.5 44.4 %tree_scan.1 = (bf16[1,256,1024]{2,1,0:T(8,128)(2,1)S(1)}, bf16[1,256,1024]{2,1,0:T(8,128)(2,1)S(1)}, f32[1,16,256]{2,1,0:T(8,128)S(1)}, bf16[1,16,1024]{2,1,0:T(8,128)(2,1)S(1)}, bf16[1,16,1024]{2,1,0:T(8,128)(2,1)S(1)}) custom-call(s32[16]{0:T(128)S(1)} %copy-done.5, f32[16]{0:T(128)S(1)} %copy-done.6, f32[16]{0:T(128)S(1)} %copy-done.7, ...), custom_call_target="tpu_custom_call" | custom-call | tf_op jit(solution)/shard_map/tree_scan/pallas_call | solution.py:424
  51.9 0.8 %copy.18 = bf16[1,256,1024]{2,1,0:T(8,128)(2,1)} copy(bf16[1,256,1024]{2,1,0:T(8,128)(2,1)S(1)} %get-tuple-element.10) | data formatting | bytes 1048576
  52.7 0.8 %copy.19 = bf16[1,256,1024]{2,1,0:T(8,128)(2,1)} copy(bf16[1,256,1024]{2,1,0:T(8,128)(2,1)S(1)} %get-tuple-element.11) | data formatting | bytes 1048576
  53.5 0.6 %copy.20 = f32[1,16,256]{2,1,0:T(8,128)} copy(f32[1,16,256]{2,1,0:T(8,128)S(1)} %get-tuple-element.12) | data formatting | bytes 32768
  54.1 0.6 %copy.21 = bf16[1,16,1024]{2,1,0:T(8,128)(2,1)} copy(bf16[1,16,1024]{2,1,0:T(8,128)(2,1)S(1)} %get-tuple-element.13) | data formatting | bytes 65536
  54.7 0.6 %copy.22 = bf16[1,16,1024]{2,1,0:T(8,128)(2,1)} copy(bf16[1,16,1024]{2,1,0:T(8,128)(2,1)S(1)} %get-tuple-element.14) | data formatting | bytes 65536
Async XLA Ops:
  0.6 1.0 %copy-start = (bf16[1,256,1024]{2,1,0:T(8,128)(2,1)S(1)}, bf16[1,256,1024]{2,1,0:T(8,128)(2,1)}, u32[]{:S(2)}) copy-start(bf16[1,256,1024]{2,1,0:T(8,128)(2,1)} %x_hbm.1) | copy-start | bytes 1572868
  1.7 1.0 %copy-start.1 = (bf16[1,256,1024]{2,1,0:T(8,128)(2,1)S(1)}, bf16[1,256,1024]{2,1,0:T(8,128)(2,1)}, u32[]{:S(2)}) copy-start(bf16[1,256,1024]{2,1,0:T(8,128)(2,1)} %dy_hbm.1) | copy-start | bytes 1572868
  2.7 1.0 %copy-start.2 = (bf16[1,256,1024]{2,1,0:T(8,128)(2,1)S(1)}, bf16[1,256,1024]{2,1,0:T(8,128)(2,1)}, u32[]{:S(2)}) copy-start(bf16[1,256,1024]{2,1,0:T(8,128)(2,1)} %b_hbm.1) | copy-start | bytes 1572868
  3.8 1.0 %copy-start.3 = (bf16[1,256,1024]{2,1,0:T(8,128)(2,1)S(1)}, bf16[1,256,1024]{2,1,0:T(8,128)(2,1)}, u32[]{:S(2)}) copy-start(bf16[1,256,1024]{2,1,0:T(8,128)(2,1)} %c_hbm.1) | copy-start | bytes 1572868
  4.8 0.7 %copy-start.4 = (f32[1,16,256]{2,1,0:T(8,128)S(1)}, f32[1,16,256]{2,1,0:T(8,128)}, u32[]{:S(2)}) copy-start(f32[1,16,256]{2,1,0:T(8,128)} %deltas_hbm.1) | copy-start | bytes 49156
  5.5 0.7 %copy-start.5 = (s32[16]{0:T(128)S(1)}, s32[16]{0:T(128)}, u32[]{:S(2)}) copy-start(s32[16]{0:T(128)} %parents.1) | copy-start | bytes 196
  6.2 0.7 %copy-start.6 = (f32[16]{0:T(128)S(1)}, f32[16]{0:T(128)}, u32[]{:S(2)}) copy-start(f32[16]{0:T(128)} %rates.1) | copy-start | bytes 196
  6.8 0.7 %copy-start.7 = (f32[16]{0:T(128)S(1)}, f32[16]{0:T(128)}, u32[]{:S(2)}) copy-start(f32[16]{0:T(128)} %skips.1) | copy-start | bytes 196

commit v2 on v1

--- a/solution.py
+++ b/solution.py
@@ -41,6 +41,11 @@
     return high, mid, (rest - mid.astype(F32)).astype(BF16)
 
 
+def nearest(i, n):
+    step = (i + 1) // 2
+    return jnp.where(lax.rem(i, 2) == 1, step, n - step)
+
+
 def sum_with(v, ones):
     high, mid, low = thirds(v)
     return dot_nn(high, ones) + (dot_nn(mid, ones) + dot_nn(low, ones))
@@ -48,12 +53,12 @@
 
 def kernel(
     heads, owners, wide,
-    parents, rates, skips, deltas_hbm, x_hbm, dy_hbm, b_hbm, c_hbm,
-    out_hbm, gx_hbm, gd_hbm, gw_hbm, gr_hbm,
+    parents_hbm, rates_hbm, skips_hbm, deltas_hbm, x_hbm, dy_hbm, b_hbm, c_hbm,
+    out_v, gx_v, gd_v, gw_v, gr_v,
     deltas, x, dy, b, c, xh, xl, yh, yl, x2, y2, e1x, e2x, y_in, h_in,
     u_buf, v_buf, a_buf, u_got, v_got, a_got, e_one, s_buf, e_buf, s_all, e_all,
-    dc_buf, db_buf, dc_got, db_got, out_v, gx_v, gd_v, gw_v, gr_v, kids, pidx, gidx,
-    in_sem, out_sem, su, ru, sv, rv, sa, ra, ss, rs, se, re, sc, rc, sb, rb,
+    em_buf, dc_buf, db_buf, dc_got, db_got, parents, rates, skips, kids, pidx, gidx,
+    in_sem, su, ru, sv, rv, sa, ra, ss, rs, se, re, sc, rc, sb, rb,
 ):
     columns = heads * P_SIZE
     rows = LENGTH // owners
@@ -71,6 +76,9 @@
         load(x_hbm.at[0], x, 2),
         load(c_hbm.at[0, :, pl.ds(group_col, N)], c, 3),
         load(dy_hbm.at[0], dy, 4),
+        load(rates_hbm, rates, 5),
+        load(parents_hbm, parents, 6),
+        load(skips_hbm, skips, 7),
     ]
     for one in loads:
         one.start()
@@ -111,6 +119,7 @@
     a_got[SEGS] = jnp.zeros((1, N), F32)
     e_one[SEGS] = jnp.zeros((half, N), F32)
 
+    loads[5].wait()
     row_h = lax.broadcasted_iota(jnp.int32, (heads, 1), 0)
     rate_col = jnp.zeros((heads, 1), F32)
     for h in range(heads):
@@ -153,35 +162,37 @@
         u_buf[:, cut] = (em_row[:, cut] * (dot_nn(bt, high) + dot_nn(bt, low))).astype(BF16)
     for z in range(SEGS // 2):
         part = em_row[:, z * N : (z + 1) * N]
+        em_buf[z] = part
         a_buf[z] = part * part
 
     pl.semaphore_wait(barrier, SEGS - 1 + owners - 1)
 
-    def seg_peer(d):
+    def seg_peer(i):
+        d = nearest(i, SEGS)
         peer = lax.rem(seg + d, SEGS)
         came = lax.rem(seg - d + SEGS, SEGS)
-        return peer, came
+        return peer, came, d
 
     def spot(ref, s):
         z, core = s // 2, lax.rem(s, 2)
         return ref.at[pl.ds(pl.multiple_of(core * half, half), half), pl.ds(pl.multiple_of(z * N, N), N)]
 
-    def up_copy(buf, got, send, recv, d, dst):
-        peer, _ = seg_peer(d)
+    def up_copy(buf, got, send, recv, i, dst):
+        peer, _, d = seg_peer(i)
         return pltpu.make_async_remote_copy(
             src_ref=spot(buf, peer), dst_ref=got.at[dst], send_sem=send.at[d], recv_sem=recv.at[d],
             device_id=(peer, head), device_id_type=MESH,
         )
 
-    def a_copy(d, dst):
-        peer, _ = seg_peer(d)
+    def a_copy(i, dst):
+        peer, _, d = seg_peer(i)
         return pltpu.make_async_remote_copy(
             src_ref=a_buf.at[peer // 2], dst_ref=a_got.at[dst], send_sem=sa.at[d], recv_sem=ra.at[d],
             device_id=(peer, head), device_id_type=MESH,
         )
 
-    def down_copy(buf, whole, send, recv, d, owner):
-        peer, _ = seg_peer(d)
+    def down_copy(buf, whole, send, recv, i, owner):
+        peer, _, d = seg_peer(i)
         return pltpu.make_async_remote_copy(
             src_ref=buf.at[peer], dst_ref=spot(whole, owner), send_sem=send.at[d], recv_sem=recv.at[d],
             device_id=(peer, head), device_id_type=MESH,
@@ -208,13 +219,8 @@
         yl[:, cut] = low
         v_buf[:, cut] = (em_row[:, cut] * (dot_nn(ct, high) + dot_nn(ct, low))).astype(BF16)
 
-    def send_v(d, carry):
-        up_copy(v_buf, v_got, sv, rv, d, seg).start()
-        return carry
-
-    lax.fori_loop(1, SEGS, send_v, 0)
-    v_got[seg] = spot(v_buf, seg)[...]
-
+    loads[6].wait()
+    loads[7].wait()
     lax.fori_loop(0, SEGS, table, 0)
     gram = jnp.where(causal, dot_nt(c[...], b[...]), 0.0)
     gram_t = jnp.where(t_row <= t_col, dot_nt(b[...], c[...]), 0.0)
@@ -235,8 +241,15 @@
     dc_buf[...] = dot_nn(kh, b[...]) + dot_nn(kl, b[...])
     db_buf[...] = dot_tn(kh, c[...]) + dot_tn(kl, c[...])
 
+    def send_v(d, carry):
+        up_copy(v_buf, v_got, sv, rv, d, seg).start()
+        return carry
+
+    lax.fori_loop(1, SEGS, send_v, 0)
+    v_got[seg] = spot(v_buf, seg)[...]
+
     def wait_u(d, carry):
-        _, came = seg_peer(d)
+        _, came, _ = seg_peer(d)
         up_copy(u_buf, u_got, su, ru, d, came).wait_recv()
         a_copy(d, came).wait_recv()
         return carry
@@ -248,7 +261,7 @@
         s_buf[s] = (a_got[p] * u_got[g].astype(F32) + u_got[p].astype(F32)).astype(BF16)
 
     def send_s(d, carry):
-        peer, _ = seg_peer(d)
+        peer, _, _ = seg_peer(d)
         start_of(peer)
         down_copy(s_buf, s_all, ss, rs, d, seg).start()
         return carry
@@ -258,7 +271,7 @@
     spot(s_all, seg)[...] = s_buf[seg]
 
     def wait_v(d, carry):
-        _, came = seg_peer(d)
+        _, came, _ = seg_peer(d)
         up_copy(v_buf, v_got, sv, rv, d, came).wait_recv()
         return carry
 
@@ -281,7 +294,7 @@
         e_buf[s] = total.astype(BF16)
 
     def send_e(d, carry):
-        peer, _ = seg_peer(d)
+        peer, _, _ = seg_peer(d)
         end_grad(peer)
         down_copy(e_buf, e_all, se, re, d, seg).start()
         return carry
@@ -297,30 +310,43 @@
             send_sem=send.at[d], recv_sem=recv.at[d], device_id=(seg, peer), device_id_type=MESH,
         )
 
-    def skip_row(at):
-        lane = lax.broadcasted_iota(jnp.int32, (1, wide), 1) // P_SIZE
-        row = jnp.zeros((1, wide), F32)
-        for h in range(wide // P_SIZE):
-            row = jnp.where(lane == h, skips[at // P_SIZE + h], row)
-        return row
-
-    def wait_s(d, carry):
-        _, came = seg_peer(d)
-        down_copy(s_buf, s_all, ss, rs, d, came).wait_recv()
-        return carry
-
-    lax.fori_loop(1, SEGS, wait_s, 0)
+    lane = lax.broadcasted_iota(jnp.int32, (1, N), 1)
+    near_rows = lax.broadcasted_iota(jnp.int32, (heads, N), 0)
+    near_lane = lax.broadcasted_iota(jnp.int32, (heads, N), 1) // P_SIZE
+
+    def zone(i):
+        z = lax.rem(my_z + nearest(i, SEGS // 2), SEGS // 2)
+        at = pl.ds(pl.multiple_of(z * N, N), N)
+        skip = jnp.where(lane < P_SIZE, skips[2 * z], skips[2 * z + 1])
+        pick = (near_rows == near_lane + 2 * z).astype(BF16)
+        return z, at, skip, pick
+
+    def wait_zone(buf, whole, send, recv, i):
+        first = 1 if i == 0 else 0
+        for core in range(first, 2):
+            if i == 0:
+                d = jnp.where(my_core == 0, 1, SEGS - 1)
+            else:
+                d = lax.rem(2 * nearest(i, SEGS // 2) + core - my_core + SEGS, SEGS)
+            came = lax.rem(seg + d, SEGS)
+            there = lax.rem(SEGS - d, SEGS)
+            pltpu.make_async_remote_copy(
+                src_ref=buf.at[came], dst_ref=spot(whole, came), send_sem=send.at[d], recv_sem=recv.at[there],
+                device_id=(came, head), device_id_type=MESH,
+            ).wait_recv()
+
     d_one = jnp.zeros((heads, LENGTH), F32)
     dc = dc_buf[...]
-    for cut in blocks:
-        core = y_in[:, cut] + e1x[:, cut] * dot_nn(c[...], s_all[:, cut])
-        out_v[:, cut] = (core + skip_row(cut.start) * x[:, cut].astype(F32)).astype(BF16)
-        high, low = halves(core * dy[:, cut].astype(F32))
-        d_one += dot_nt(pick1[:, cut], high) + dot_nt(pick1[:, cut], low)
-        dc += dot_nt(y2[:, cut], s_all[:, cut])
+    for i in range(SEGS // 2):
+        wait_zone(s_buf, s_all, ss, rs, i)
+        z, at, skip, pick = zone(i)
+        starts = s_all[:, at]
+        core = y_in[:, at] + e1x[:, at] * dot_nn(c[...], starts)
+        out_v[0, :, at] = (core + skip * x[:, at].astype(F32)).astype(BF16)
+        high, low = halves(core * dy[:, at].astype(F32))
+        d_one += dot_nt(pick, high) + dot_nt(pick, low)
+        dc += dot_nt(y2[:, at], starts)
     dc_buf[...] = dc
-    out_copy = pltpu.make_async_copy(out_v, out_hbm.at[0], out_sem.at[0])
-    out_copy.start()
 
     def send_dc(d, carry):
         head_copy(dc_buf, dc_got, sc, rc, d, head).start()
@@ -329,29 +355,24 @@
     lax.fori_loop(1, owners, send_dc, 0)
     dc_got[head] = dc_buf[pl.ds(pl.multiple_of(head * rows, rows), rows)]
 
-    def wait_e(d, carry):
-        _, came = seg_peer(d)
-        down_copy(e_buf, e_all, se, re, d, came).wait_recv()
-        return carry
-
-    lax.fori_loop(1, SEGS, wait_e, 0)
     d_two = jnp.zeros((heads, LENGTH), F32)
     d_last = jnp.zeros((heads, 8), F32)
     db = db_buf[...]
-    for cut in blocks:
-        ends = e_all[:, cut]
-        x_cut = x[:, cut].astype(F32)
-        late = e2x[:, cut] * dot_nn(b[...], ends)
-        grad = h_in[:, cut] + late
-        gx_v[:, cut] = (grad + skip_row(cut.start) * dy[:, cut].astype(F32)).astype(BF16)
+    for i in range(SEGS // 2):
+        wait_zone(e_buf, e_all, se, re, i)
+        z, at, skip, pick = zone(i)
+        ends = e_all[:, at]
+        x_cut = x[:, at].astype(F32)
+        late = e2x[:, at] * dot_nn(b[...], ends)
+        grad = h_in[:, at] + late
+        gx_v[0, :, at] = (grad + skip * dy[:, at].astype(F32)).astype(BF16)
         high, low = halves(grad * x_cut)
-        d_two += dot_nt(pick1[:, cut], high) + dot_nt(pick1[:, cut], low)
-        em = em_row[:, cut]
-        both = jnp.sum(ends.astype(F32) * s_all[:, cut].astype(F32), axis=0, keepdims=True)
-        tail = jnp.sum(late * x_cut, axis=0, keepdims=True) + em * em * both
-        high, low = halves(jnp.broadcast_to(tail, (8, wide)))
-        d_last += dot_nt(pick1[:, cut], high) + dot_nt(pick1[:, cut], low)
-        db += dot_nt(x2[:, cut], ends)
+        d_two += dot_nt(pick, high) + dot_nt(pick, low)
+        both = jnp.sum(ends.astype(F32) * s_all[:, at].astype(F32), axis=0, keepdims=True)
+        tail = jnp.sum(late * x_cut, axis=0, keepdims=True) + a_buf[z] * both
+        high, low = halves(jnp.broadcast_to(tail, (8, N)))
+        d_last += dot_nt(pick, high) + dot_nt(pick, low)
+        db += dot_nt(x2[:, at], ends)
     db_buf[...] = db
 
     def send_db(d, carry):
@@ -360,14 +381,10 @@
 
     lax.fori_loop(1, owners, send_db, 0)
     db_got[head] = db_buf[pl.ds(pl.multiple_of(head * rows, rows), rows)]
-    gx_copy = pltpu.make_async_copy(gx_v, gx_hbm.at[0], out_sem.at[1])
-    gx_copy.start()
 
     since = (t_row >= t_col).astype(BF16)
     later = sum_with(d_one - d_two, since) + d_last[:, :1]
-    gd_v[...] = d_two / delta - rate_col * later
-    gd_copy = pltpu.make_async_copy(gd_v, gd_hbm.at[0], out_sem.at[2])
-    gd_copy.start()
+    gd_v[0] = d_two / delta - rate_col * later
 
     share = max(1, HEADS_PER_GROUP // heads)
 
@@ -381,14 +398,10 @@
             total = got[g * share]
             for k in range(1, share):
                 total += got[g * share + k]
-            dst[:, g * N : (g + 1) * N] = total.astype(BF16)
+            dst[0, :, g * N : (g + 1) * N] = total.astype(BF16)
 
     finish(dc_got, dc_buf, sc, rc, gr_v)
-    gr_copy = pltpu.make_async_copy(gr_v, gr_hbm.at[0], out_sem.at[3])
-    gr_copy.start()
     finish(db_got, db_buf, sb, rb, gw_v)
-    gw_copy = pltpu.make_async_copy(gw_v, gw_hbm.at[0], out_sem.at[4])
-    gw_copy.start()
 
     def drain_seg(d, carry):
         up_copy(u_buf, u_got, su, ru, d, seg).wait_send()
@@ -405,7 +418,15 @@
 
     lax.fori_loop(1, SEGS, drain_seg, 0)
     lax.fori_loop(1, owners, drain_head, 0)
-    for one in (out_copy, gx_copy, gd_copy, gr_copy, gw_copy):
+
+
+def store(*refs):
+    sems = refs[-1]
+    done = len(refs) // 2
+    copies = [pltpu.make_async_copy(refs[k], refs[done + k], sems.at[k]) for k in range(done)]
+    for one in copies:
+        one.start()
+    for one in copies:
         one.wait()
 
 
@@ -418,38 +439,47 @@
     wide_b = lambda: vm((LENGTH, columns), BF16)
     wide_f = lambda: vm((LENGTH, columns), F32)
     sem = lambda n: pltpu.SemaphoreType.DMA((n,))
-    anywhere = pl.BlockSpec(memory_space=pl.ANY)
-    scalars = pl.BlockSpec(memory_space=pltpu.SMEM)
+    anywhere = pl.BlockSpec(memory_space=pltpu.HBM)
+    vectors = pl.BlockSpec(memory_space=pltpu.VMEM)
+    results = (
+        jax.ShapeDtypeStruct(inputs.shape, BF16),
+        jax.ShapeDtypeStruct(inputs.shape, BF16),
+        jax.ShapeDtypeStruct(deltas.shape, F32),
+        jax.ShapeDtypeStruct((1, rows, writer.shape[2]), BF16),
+        jax.ShapeDtypeStruct((1, rows, writer.shape[2]), BF16),
+    )
+    made = pl.pallas_call(
+        functools.partial(kernel, heads, owners, 256),
+        out_shape=results,
+        in_specs=[anywhere] * 8,
+        out_specs=[vectors] * 5,
+        scratch_shapes=[
+            vm((heads, LENGTH), F32), wide_b(), wide_b(), vm((LENGTH, N), BF16), vm((LENGTH, N), BF16),
+            wide_b(), wide_b(), wide_b(), wide_b(), wide_b(), wide_b(), wide_f(), wide_f(), wide_f(), wide_f(),
+            vm((N, columns), BF16), vm((N, columns), BF16), vm((SEGS // 2, 1, N), F32),
+            vm((SEGS + 1, half, N), BF16), vm((SEGS + 1, half, N), BF16), vm((SEGS + 1, 1, N), F32),
+            vm((SEGS + 1, half, N), F32), vm((SEGS, half, N), BF16), vm((SEGS, half, N), BF16),
+            vm((N, columns), BF16), vm((N, columns), BF16), vm((SEGS // 2, 1, N), F32),
+            vm((LENGTH, N), F32), vm((LENGTH, N), F32), vm((owners, rows, N), F32), vm((owners, rows, N), F32),
+            pltpu.SMEM((SEGS,), jnp.int32), pltpu.SMEM((heads,), F32), pltpu.SMEM((heads,), F32),
+            pltpu.SMEM((KIDS * SEGS,), jnp.int32), pltpu.SMEM((SEGS,), jnp.int32), pltpu.SMEM((SEGS,), jnp.int32),
+            sem(8),
+        ] + [sem(SEGS)] * 10 + [sem(owners)] * 4,
+        compiler_params=pltpu.CompilerParams(
+            collective_id=0, has_side_effects=True, vmem_limit_bytes=48 * 1024 * 1024
+        ),
+        name="tree_scan",
+    )(*(pltpu.with_memory_space_constraint(a, pltpu.HBM) for a in (parents, rates, skips, deltas, inputs, grad_out, writer, reader)))
     return tuple(
         pl.pallas_call(
-            functools.partial(kernel, heads, owners, 256),
-            out_shape=(
-                jax.ShapeDtypeStruct(inputs.shape, BF16),
-                jax.ShapeDtypeStruct(inputs.shape, BF16),
-                jax.ShapeDtypeStruct(deltas.shape, F32),
-                jax.ShapeDtypeStruct((1, rows, writer.shape[2]), BF16),
-                jax.ShapeDtypeStruct((1, rows, writer.shape[2]), BF16),
-            ),
-            in_specs=[scalars] * 3 + [anywhere] * 5,
+            store,
+            out_shape=results,
+            in_specs=[vectors] * 5,
             out_specs=[anywhere] * 5,
-            scratch_shapes=[
-                vm((heads, LENGTH), F32), wide_b(), wide_b(), vm((LENGTH, N), BF16), vm((LENGTH, N), BF16),
-                wide_b(), wide_b(), wide_b(), wide_b(), wide_b(), wide_b(), wide_f(), wide_f(), wide_f(), wide_f(),
-                vm((N, columns), BF16), vm((N, columns), BF16), vm((SEGS // 2, 1, N), F32),
-                vm((SEGS + 1, half, N), BF16), vm((SEGS + 1, half, N), BF16), vm((SEGS + 1, 1, N), F32),
-                vm((SEGS + 1, half, N), F32), vm((SEGS, half, N), BF16), vm((SEGS, half, N), BF16),
-                vm((N, columns), BF16), vm((N, columns), BF16),
-                vm((LENGTH, N), F32), vm((LENGTH, N), F32), vm((owners, rows, N), F32), vm((owners, rows, N), F32),
-                wide_b(), wide_b(), vm((heads, LENGTH), F32),
-                vm((rows, writer.shape[2]), BF16), vm((rows, writer.shape[2]), BF16),
-                pltpu.SMEM((KIDS * SEGS,), jnp.int32), pltpu.SMEM((SEGS,), jnp.int32), pltpu.SMEM((SEGS,), jnp.int32),
-                sem(5), sem(5),
-            ] + [sem(SEGS)] * 10 + [sem(owners)] * 4,
-            compiler_params=pltpu.CompilerParams(
-                collective_id=0, has_side_effects=True, vmem_limit_bytes=48 * 1024 * 1024
-            ),
-            name="tree_scan",
-        )(parents, rates, skips, deltas, inputs, grad_out, writer, reader)
+            scratch_shapes=[sem(5)],
+            compiler_params=pltpu.CompilerParams(vmem_limit_bytes=32 * 1024 * 1024),
+            name="store",
+        )(*made)
     )
 
 

time: 55.7 us -> 44.5 us (0.80)
  local copies, waits for them, and re-layouts: 10.3 us -> 0 us
  Pallas kernels: 44.4 us -> 43.8 us
    unnamed x21 -> x0, local copies, waits for them, and re-layouts: 10.3 us -> none
    pallas_call x1 -> x2, Pallas kernels: 44.4 us -> 43.8 us  [the longest x1 42.7 us: shards(): pl.pallas_call(functools.partial(kernel, heads, owners, 256), out_shape=r...]
where the time goes in v2:
time: 44.5 us; the launch traced here: 44.4 us
  Pallas kernels  43.8 us (98%)
  between operations  0.64 us (1%)
    pallas_call x1, Pallas kernels, shards(): pl.pallas_call(functools.partial(kernel, heads, owners, 256), out_shape=r...  42.7 us
    pallas_call x1, Pallas kernels, shards(): pl.pallas_call(store, out_shape=results, in_specs=[vectors] * 5, out_spec...  1.02 us

profile of v2, /device:TPU:1, one launch (start us, length us, event | category | flops | bytes accessed | tf_op | source)
XLA Modules:
  0.0 44.4 jit_solution(11369480718105174821)
XLA Ops:
  0.6 42.7 %tree_scan.1 = (bf16[1,256,1024]{2,1,0:T(8,128)(2,1)S(1)}, bf16[1,256,1024]{2,1,0:T(8,128)(2,1)S(1)}, f32[1,16,256]{2,1,0:T(8,128)S(1)}, bf16[1,16,1024]{2,1,0:T(8,128)(2,1)S(1)}, bf16[1,16,1024]{2,1,0:T(8,128)(2,1)S(1)}) custom-call(s32[16]{0:T(128)} %parents_hbm.1, f32[16]{0:T(128)} %rates_hbm.1, f32[16]{0:T(128)} %skips_hbm.1, f32[1,16,256]{2,1,0:T(8,128)} %deltas_hbm.1, ...), custom_call_target="tpu_custom_call" | custom-call | tf_op jit(solution)/shard_map/tree_scan/pallas_call | solution.py:451
  43.4 1.0 %store.1 = (bf16[1,256,1024]{2,1,0:T(8,128)(2,1)}, bf16[1,256,1024]{2,1,0:T(8,128)(2,1)}, f32[1,16,256]{2,1,0:T(8,128)}, bf16[1,16,1024]{2,1,0:T(8,128)(2,1)}, bf16[1,16,1024]{2,1,0:T(8,128)(2,1)}) custom-call(bf16[1,256,1024]{2,1,0:T(8,128)(2,1)S(1)} %get-tuple-element.10.refs_0_, bf16[1,256,1024]{2,1,0:T(8,128)(2,1)S(1)} %get-tuple-element.11.refs_1_, ...), custom_call_target="tpu_custom_call" | custom-call | tf_op jit(solution)/shard_map/store/pallas_call | solution.py:474

commit v3 on v2

--- a/solution.py
+++ b/solution.py
@@ -55,9 +55,9 @@
     heads, owners, wide,
     parents_hbm, rates_hbm, skips_hbm, deltas_hbm, x_hbm, dy_hbm, b_hbm, c_hbm,
     out_v, gx_v, gd_v, gw_v, gr_v,
-    deltas, x, dy, b, c, xh, xl, yh, yl, x2, y2, e1x, e2x, y_in, h_in,
+    deltas, x, dy, b, c, xh, xl, yh, yl, x2, x2l, y2, e1x, e2x, y_in, h_in,
     u_buf, v_buf, a_buf, u_got, v_got, a_got, e_one, s_buf, e_buf, s_all, e_all,
-    em_buf, dc_buf, db_buf, dc_got, db_got, parents, rates, skips, kids, pidx, gidx,
+    em_buf, dc_buf, db_buf, db_low, dc_got, db_got, parents, rates, skips, kids, pidx, gidx,
     in_sem, su, ru, sv, rv, sa, ra, ss, rs, se, re, sc, rc, sb, rb,
 ):
     columns = heads * P_SIZE
@@ -149,23 +149,10 @@
 
     blocks = [slice(k, k + wide) for k in range(0, columns, wide)]
 
-    loads[1].wait()
-    loads[2].wait()
-    bt = b[...].T
-    for cut in blocks:
-        ex = dot_tn(e2s, pick2[:, cut])
-        e2x[:, cut] = ex
-        scaled = ex * x[:, cut].astype(F32)
-        high, low = halves(scaled)
-        xh[:, cut] = high
-        xl[:, cut] = low
-        u_buf[:, cut] = (em_row[:, cut] * (dot_nn(bt, high) + dot_nn(bt, low))).astype(BF16)
     for z in range(SEGS // 2):
         part = em_row[:, z * N : (z + 1) * N]
         em_buf[z] = part
         a_buf[z] = part * part
-
-    pl.semaphore_wait(barrier, SEGS - 1 + owners - 1)
 
     def seg_peer(i):
         d = nearest(i, SEGS)
@@ -198,14 +185,37 @@
             device_id=(peer, head), device_id_type=MESH,
         )
 
-    def send_u(d, carry):
-        up_copy(u_buf, u_got, su, ru, d, seg).start()
-        a_copy(d, seg).start()
-        return carry
-
-    lax.fori_loop(1, SEGS, send_u, 0)
-    u_got[seg] = spot(u_buf, seg)[...]
-    a_got[seg] = a_buf[my_z]
+    part_row = lax.rem(lax.broadcasted_iota(jnp.int32, (2 * heads, N), 0), heads)
+    part_lane = lax.broadcasted_iota(jnp.int32, (2 * heads, N), 1) // P_SIZE
+    loads[1].wait()
+    bt = b[...].T
+    loads[2].wait()
+    for i in range(SEGS // 2):
+        ahead = nearest(i, SEGS // 2) if i else 0
+        z = lax.rem(my_z + ahead, SEGS // 2)
+        at = pl.ds(pl.multiple_of(z * N, N), N)
+        ex = dot_tn(e2s, (part_row == part_lane + 2 * z).astype(BF16))
+        e2x[:, at] = ex
+        scaled = ex * x[:, at].astype(F32)
+        high, low = halves(scaled)
+        xh[:, at] = high
+        xl[:, at] = low
+        u_buf[:, at] = (em_buf[z] * (dot_nn(bt, high) + dot_nn(bt, low))).astype(BF16)
+        if i == 0:
+            pl.semaphore_wait(barrier, SEGS - 1 + owners - 1)
+            u_got[seg] = spot(u_buf, seg)[...]
+            a_got[seg] = a_buf[my_z]
+        for core in range(1 if i == 0 else 0, 2):
+            peer = seg + 1 - 2 * my_core if i == 0 else 2 * z + core
+            d = lax.rem(peer - seg + SEGS, SEGS)
+            pltpu.make_async_remote_copy(
+                src_ref=spot(u_buf, peer), dst_ref=u_got.at[seg], send_sem=su.at[d], recv_sem=ru.at[d],
+                device_id=(peer, head), device_id_type=MESH,
+            ).start()
+            pltpu.make_async_remote_copy(
+                src_ref=a_buf.at[z], dst_ref=a_got.at[seg], send_sem=sa.at[d], recv_sem=ra.at[d],
+                device_id=(peer, head), device_id_type=MESH,
+            ).start()
 
     loads[3].wait()
     loads[4].wait()
@@ -234,7 +244,9 @@
         k_sum += dot_nt(y_high, x_high) + (dot_nt(y_high, x_low) + dot_nt(y_low, x_high))
         e1x[:, cut] = e1x[:, cut] * em_row[:, cut]
         e2x[:, cut] = e2x[:, cut] * em_row[:, cut]
-        x2[:, cut] = (e2x[:, cut] * x[:, cut].astype(F32)).astype(BF16)
+        high, low = halves(e2x[:, cut] * x[:, cut].astype(F32))
+        x2[:, cut] = high
+        x2l[:, cut] = low
         y2[:, cut] = (e1x[:, cut] * dy[:, cut].astype(F32)).astype(BF16)
     k_sum = jnp.where(causal, k_sum, 0.0)
     kh, kl = halves(k_sum)
@@ -372,15 +384,15 @@
         tail = jnp.sum(late * x_cut, axis=0, keepdims=True) + a_buf[z] * both
         high, low = halves(jnp.broadcast_to(tail, (8, N)))
         d_last += dot_nt(pick, high) + dot_nt(pick, low)
-        db += dot_nt(x2[:, at], ends)
-    db_buf[...] = db
+        db += dot_nt(x2[:, at], ends) + dot_nt(x2l[:, at], ends)
+    db_low[...] = db.astype(BF16)
 
     def send_db(d, carry):
-        head_copy(db_buf, db_got, sb, rb, d, head).start()
+        head_copy(db_low, db_got, sb, rb, d, head).start()
         return carry
 
     lax.fori_loop(1, owners, send_db, 0)
-    db_got[head] = db_buf[pl.ds(pl.multiple_of(head * rows, rows), rows)]
+    db_got[head] = db_low[pl.ds(pl.multiple_of(head * rows, rows), rows)]
 
     since = (t_row >= t_col).astype(BF16)
     later = sum_with(d_one - d_two, since) + d_last[:, :1]
@@ -395,13 +407,15 @@
 
         lax.fori_loop(1, owners, wait_one, 0)
         for g in range(owners // share):
-            total = got[g * share]
+            total = got[g * share].astype(F32)
             for k in range(1, share):
-                total += got[g * share + k]
+                total += got[g * share + k].astype(F32)
             dst[0, :, g * N : (g + 1) * N] = total.astype(BF16)
 
     finish(dc_got, dc_buf, sc, rc, gr_v)
-    finish(db_got, db_buf, sb, rb, gw_v)
+    def drain_dc(d, carry):
+        head_copy(dc_buf, dc_got, sc, rc, d, head).wait_send()
+        return carry
 
     def drain_seg(d, carry):
         up_copy(u_buf, u_got, su, ru, d, seg).wait_send()
@@ -411,12 +425,15 @@
         down_copy(e_buf, e_all, se, re, d, seg).wait_send()
         return carry
 
+    lax.fori_loop(1, owners, drain_dc, 0)
+    lax.fori_loop(1, SEGS, drain_seg, 0)
+
+    finish(db_got, db_low, sb, rb, gw_v)
+
     def drain_head(d, carry):
-        head_copy(dc_buf, dc_got, sc, rc, d, head).wait_send()
-        head_copy(db_buf, db_got, sb, rb, d, head).wait_send()
-        return carry
-
-    lax.fori_loop(1, SEGS, drain_seg, 0)
+        head_copy(db_low, db_got, sb, rb, d, head).wait_send()
+        return carry
+
     lax.fori_loop(1, owners, drain_head, 0)
 
 
@@ -455,12 +472,12 @@
         out_specs=[vectors] * 5,
         scratch_shapes=[
             vm((heads, LENGTH), F32), wide_b(), wide_b(), vm((LENGTH, N), BF16), vm((LENGTH, N), BF16),
-            wide_b(), wide_b(), wide_b(), wide_b(), wide_b(), wide_b(), wide_f(), wide_f(), wide_f(), wide_f(),
+            wide_b(), wide_b(), wide_b(), wide_b(), wide_b(), wide_b(), wide_b(), wide_f(), wide_f(), wide_f(), wide_f(),
             vm((N, columns), BF16), vm((N, columns), BF16), vm((SEGS // 2, 1, N), F32),
             vm((SEGS + 1, half, N), BF16), vm((SEGS + 1, half, N), BF16), vm((SEGS + 1, 1, N), F32),
             vm((SEGS + 1, half, N), F32), vm((SEGS, half, N), BF16), vm((SEGS, half, N), BF16),
             vm((N, columns), BF16), vm((N, columns), BF16), vm((SEGS // 2, 1, N), F32),
-            vm((LENGTH, N), F32), vm((LENGTH, N), F32), vm((owners, rows, N), F32), vm((owners, rows, N), F32),
+            vm((LENGTH, N), F32), vm((LENGTH, N), F32), vm((LENGTH, N), BF16), vm((owners, rows, N), F32), vm((owners, rows, N), BF16),
             pltpu.SMEM((SEGS,), jnp.int32), pltpu.SMEM((heads,), F32), pltpu.SMEM((heads,), F32),
             pltpu.SMEM((KIDS * SEGS,), jnp.int32), pltpu.SMEM((SEGS,), jnp.int32), pltpu.SMEM((SEGS,), jnp.int32),
             sem(8),

time: 44.5 us -> 44.7 us (level)
  no operation moved by 1% of the time
where the time goes in v3:
time: 44.7 us; the launch traced here: 44.6 us
  Pallas kernels  43.9 us (98%)
  between operations  0.64 us (1%)
    pallas_call x1, Pallas kernels, shards(): pl.pallas_call(functools.partial(kernel, heads, owners, 256), out_shape=r...  42.9 us
    pallas_call x1, Pallas kernels, shards(): pl.pallas_call(store, out_shape=results, in_specs=[vectors] * 5, out_spec...  1.02 us

profile of v3, /device:TPU:1, one launch (start us, length us, event | category | flops | bytes accessed | tf_op | source)
XLA Modules:
  0.0 44.6 jit_solution(1920047348753330061)
XLA Ops:
  0.6 42.9 %tree_scan.1 = (bf16[1,256,1024]{2,1,0:T(8,128)(2,1)S(1)}, bf16[1,256,1024]{2,1,0:T(8,128)(2,1)S(1)}, f32[1,16,256]{2,1,0:T(8,128)S(1)}, bf16[1,16,1024]{2,1,0:T(8,128)(2,1)S(1)}, bf16[1,16,1024]{2,1,0:T(8,128)(2,1)S(1)}) custom-call(s32[16]{0:T(128)} %parents_hbm.1, f32[16]{0:T(128)} %rates_hbm.1, f32[16]{0:T(128)} %skips_hbm.1, f32[1,16,256]{2,1,0:T(8,128)} %deltas_hbm.1, ...), custom_call_target="tpu_custom_call" | custom-call | tf_op jit(solution)/shard_map/tree_scan/pallas_call | solution.py:468
  43.6 1.0 %store.1 = (bf16[1,256,1024]{2,1,0:T(8,128)(2,1)}, bf16[1,256,1024]{2,1,0:T(8,128)(2,1)}, f32[1,16,256]{2,1,0:T(8,128)}, bf16[1,16,1024]{2,1,0:T(8,128)(2,1)}, bf16[1,16,1024]{2,1,0:T(8,128)(2,1)}) custom-call(bf16[1,256,1024]{2,1,0:T(8,128)(2,1)S(1)} %get-tuple-element.10.refs_0_, bf16[1,256,1024]{2,1,0:T(8,128)(2,1)S(1)} %get-tuple-element.11.refs_1_, ...), custom_call_target="tpu_custom_call" | custom-call | tf_op jit(solution)/shard_map/store/pallas_call | solution.py:491
